TPU v7x, 512 devices: a whole 4x4x16 slice. The times are simulated.
512 devices in a mesh: rep: 4 (over y), exp: 128 (over x, z, core).
Axes of the slice: x: 4, y: 4, z: 16, core: 2. Of those that a mesh axis runs over, the one named last changes fastest.
Arguments:
- tokens: bfloat16 [16384, 3584], P(('rep', 'exp')), parts along dimension 0, may hold values from -6 to 6
- expert_ids: int32 [16384, 8], P(('rep', 'exp')), parts along dimension 0, may hold values from 0 to 383, all different within a row; in each aligned block of 32 rows (0 to 31, 32 to 63, ...) at most 2 rows name the same one
- gate_scores: float32 [16384, 8], P(('rep', 'exp')), parts along dimension 0, may hold values from 0.02 to 0.4
- gate_weight: bfloat16 [3584, 16384], P(None, 'exp'), may hold values from -0.09375 to 0.09375
- up_weight: bfloat16 [3584, 16384], P(None, 'exp'), may hold values from -0.09375 to 0.09375
- down_weight: bfloat16 [16384, 3584], P('exp'), may hold values from -0.125 to 0.125
Outputs:
- combined: bfloat16 [16384, 3584], P(('rep', 'exp')), parts along dimension 0
- expert_load: float32 [1536], P('rep'), parts along dimension 0
There are 4 independent parts, one for each index of `rep`. A program takes and returns all parts, laid end to end along the dimension named above; an argument that names none is the same for every part. Nothing has to cross between parts.
Inputs may be any that keep to these rules, and one draw needn't show every extreme that they name: `expert_ids`: each row names 8 different experts. Among the rows of one device no expert is named by more than 2 rows, a bound that some block reaches.
All inputs are finite; a program needn't handle non-finite values.
Results may differ from a plain program's by a relative error of at most 0.0057.
Values may be sent and summed in bfloat16 or wider, within the bound.
No kernel may reach another device: no remote copies, remote signals or barrier semaphores. Data moves between devices by JAX's collectives and lax.ppermute only.
A program may use at most 64 MiB of HBM per device.

v0:
```python
import jax
import jax.numpy as jnp
from jax import lax
from jax.sharding import PartitionSpec as P

FF = 2048
EXPERTS_ALL = 384
EXPERTS = 8
CAP = 2


def expert_rows(arrived, gate_weight, up_weight, down_weight):
    flat_rows = arrived.reshape(-1, arrived.shape[-1])
    gate_act = jnp.dot(flat_rows, gate_weight, preferred_element_type=jnp.float32)
    up_act = jnp.dot(flat_rows, up_weight, preferred_element_type=jnp.float32)
    hidden = (jax.nn.silu(gate_act) * up_act).astype(jnp.bfloat16)
    partial_value = jnp.dot(hidden, down_weight, preferred_element_type=jnp.float32).astype(
        jnp.bfloat16
    )
    return partial_value.reshape(arrived.shape)


def shards(tokens, expert_ids, gate_scores, gate_weight, up_weight, down_weight):
    dev_count = lax.axis_size("exp")
    hid_dev = gate_weight.shape[1]
    spread = FF // hid_dev
    tok_rows = tokens.shape[0]
    feat_width = tokens.shape[1]
    matches = expert_ids[:, :, None] == jnp.arange(EXPERTS_ALL, dtype=jnp.int32)[None, None, :]
    onehot = jnp.where(matches, 1.0, 0.0).astype(jnp.float32)
    routed_mass = jnp.einsum("tk,tke->e", gate_scores, onehot, precision=lax.Precision.HIGHEST)
    expert_load = lax.psum(routed_mass, "exp")
    window_match = matches[:, :, :EXPERTS]
    win_hits = jnp.any(window_match, axis=1)
    win_gate = jnp.sum(jnp.where(window_match, gate_scores[:, :, None], 0.0), axis=1)
    position = jnp.cumsum(win_hits.astype(jnp.int32), axis=0) - 1
    slot_ids = jnp.arange(CAP, dtype=jnp.int32)
    placed = win_hits[:, :, None] & (position[:, :, None] == slot_ids[None, None, :])
    placing = placed.reshape(tok_rows, EXPERTS * CAP)
    picker = jnp.where(placing.T, 1.0, 0.0).astype(jnp.bfloat16)
    outgoing = jnp.dot(picker, tokens, preferred_element_type=jnp.float32).astype(jnp.bfloat16)
    outgoing = jnp.broadcast_to(
        outgoing.reshape(EXPERTS, 1, CAP, feat_width), (EXPERTS, spread, CAP, feat_width)
    )
    outgoing = outgoing.reshape(dev_count, CAP, feat_width)
    arrived = lax.all_to_all(outgoing, "exp", split_axis=0, concat_axis=0, tiled=True)
    returned = lax.all_to_all(
        expert_rows(arrived, gate_weight, up_weight, down_weight),
        "exp",
        split_axis=0,
        concat_axis=0,
        tiled=True,
    )
    summed = jnp.sum(returned.reshape(EXPERTS, spread, CAP, feat_width), axis=1, dtype=jnp.float32)
    summed = summed.reshape(EXPERTS * CAP, feat_width)
    weights_slot = jnp.where(placed, win_gate[:, :, None], 0.0).reshape(tok_rows, EXPERTS * CAP)
    combined = jnp.dot(weights_slot, summed, precision=lax.Precision.HIGHEST).astype(jnp.bfloat16)
    return (combined, expert_load)


def solution(mesh):
    return jax.shard_map(
        shards,
        mesh=mesh,
        in_specs=(
            P(("rep", "exp"), None),
            P(("rep", "exp"), None),
            P(("rep", "exp"), None),
            P(None, "exp"),
            P(None, "exp"),
            P("exp", None),
        ),
        out_specs=(P(("rep", "exp"), None), P("rep")),
        check_vma=False,
    )
```

profile of v0, /device:TPU:1, one launch (start us, length us, event | category | flops | bytes accessed | tf_op | source)
XLA Modules:
  0.0 458.2 jit_solution(18036229864362332462)
XLA Ops:
  0.6 0.0 copy-start
  0.7 0.1 eq.45
  0.7 1.0 iota_compare_fusion
  1.8 0.1 copy.23
  1.8 0.1 reduce_window_sum.11
  1.9 0.1 copy.24
  2.0 1.2 convolution_convert_fusion.1
  3.2 0.9 broadcast_in_dim.61
  4.2 108.1 %all_to_all.10 = bf16[128,2,3584]{2,1,0:T(2,128)(2,1)} all-to-all(bf16[128,2,3584]{2,1,0:T(2,128)(2,1)S(1)} %bitcast.21), channel_id=1, replica_groups=mesh['rep'=4,'exp'=128] {'exp'}, dimensions={0} | all-to-all | bytes 3670016 | tf_op jit(solution)/shard_map/all_to_all | solution.py:46
  112.3 4.1 reshape.38
  116.4 1.8 fusion.25
  118.2 0.0 copy-done
  118.2 3.6 convolution_convert_fusion
  121.8 4.7 %reshape.39 = bf16[128,2,3584]{2,1,0:T(2,128)(2,1)} reshape(bf16[256,3584]{1,0:T(8,128)(2,1)} %convolution_convert_fusion) | data formatting | bytes 3670016 | tf_op jit(solution)/shard_map/reshape | solution.py:20
  126.6 0.0 copy-start.1
  126.6 0.0 copy-start.2
  126.6 8.9 %all-to-all-start.1 = ((bf16[128,2,3584]{2,1,0:T(2,128)(2,1)}), bf16[128,2,3584]{2,1,0:T(2,128)(2,1)S(1)}, u32[]{:S(2)}, u32[]{:S(2)}) async-start(bf16[128,2,3584]{2,1,0:T(2,128)(2,1)} %reshape.39), calls=%async_computation.1 | async-start | bytes 3670016 | tf_op jit(solution)/shard_map/all_to_all | solution.py:47
  135.4 0.0 copy-done.1
  135.4 0.0 copy-done.2
  135.4 1.5 fusion.4
  137.0 318.4 %psum.7 = f32[384]{0:T(512)} all-reduce(f32[384]{0:T(512)S(1)} %fusion.4), channel_id=1, replica_groups=mesh['rep'=4,'exp'=128] {'exp'}, use_global_device_ids=true, to_apply=%region_4.5 | all-reduce | flops 384 | bytes 3072 | tf_op jit(solution)/shard_map/psum | solution.py:32
  455.4 0.0 all-to-all-done.1
  455.4 1.5 convert_reduce_fusion
  456.9 1.3 fusion
  (10 shorter events, 0.1 us)
Async XLA Ops:
  0.6 117.6 %copy-start = (bf16[128,3584]{1,0:T(8,128)(2,1)S(1)}, bf16[128,3584]{1,0:T(8,128)(2,1)}, u32[]{:S(2)}) copy-start(bf16[128,3584]{1,0:T(8,128)(2,1)} %param.11) | copy-start | bytes 2752516
  126.6 8.9 %copy-start.1 = (s32[32,8]{0,1:T(8,128)S(1)}, s32[32,8]{0,1:T(8,128)}, u32[]{:S(2)}) copy-start(s32[32,8]{0,1:T(8,128)} %param.7) | copy-start | bytes 3076
  126.6 8.9 %copy-start.2 = (f32[32,8]{0,1:T(8,128)S(1)}, f32[32,8]{0,1:T(8,128)}, u32[]{:S(2)}) copy-start(f32[32,8]{0,1:T(8,128)} %param.8) | copy-start | bytes 3076
  126.6 328.9 %all-to-all-start.1 = ((bf16[128,2,3584]{2,1,0:T(2,128)(2,1)}), bf16[128,2,3584]{2,1,0:T(2,128)(2,1)S(1)}, u32[]{:S(2)}, u32[]{:S(2)}) async-start(bf16[128,2,3584]{2,1,0:T(2,128)(2,1)} %reshape.39), calls=%async_computation.1 | async-start | bytes 3670016 | tf_op jit(solution)/shard_map/all_to_all | solution.py:47
where the time goes:
time: 459 us; the launch traced here: 458 us
  blocking collectives  427 us (93%)
  local copies, waits for them, and re-layouts  10.1 us (2%)
  matrix products  9.36 us (2%)
  starting transfers between devices  8.85 us (2%)
    psum x1, blocking collectives, shards(): expert_load = lax.psum(routed_mass, 'exp')  318 us
    all_to_all x1, blocking collectives, shards(): lax.all_to_all(outgoing, 'exp', split_axis=0, concat_axis=0, tiled=True)  108 us
  transfers between devices with their start and end apart: 1, of which 0 were waited for; matrix products, arithmetic and copies ran while one was open for 0% of the time, Pallas kernels for 0%

commit v1 on v0

--- a/solution.py
+++ b/solution.py
@@ -29,7 +29,7 @@
     matches = expert_ids[:, :, None] == jnp.arange(EXPERTS_ALL, dtype=jnp.int32)[None, None, :]
     onehot = jnp.where(matches, 1.0, 0.0).astype(jnp.float32)
     routed_mass = jnp.einsum("tk,tke->e", gate_scores, onehot, precision=lax.Precision.HIGHEST)
-    expert_load = lax.psum(routed_mass, "exp")
+    expert_load = jnp.sum(lax.all_gather(routed_mass, "exp"), axis=0)
     window_match = matches[:, :, :EXPERTS]
     win_hits = jnp.any(window_match, axis=1)
     win_gate = jnp.sum(jnp.where(window_match, gate_scores[:, :, None], 0.0), axis=1)

time: 459 us -> 311 us (0.68)
  blocking collectives: 427 us -> 278 us
    psum x1 -> x0, blocking collectives: 318 us -> none  [shards(): expert_load = lax.psum(routed_mass, 'exp')]
    all_gather x0 -> x1, blocking collectives: none -> 170 us  [shards(): expert_load = jnp.sum(lax.all_gather(routed_mass, 'exp'), axis=0)]
  transfers between devices with their start and end apart: 1 -> 1, of which waited for: 0 -> 0; matrix products, arithmetic and copies ran while one was open for 0% -> 1% of each run, Pallas kernels for 0% -> 0%
where the time goes in v1:
time: 311 us
  blocking collectives  278 us (89%)
  local copies, waits for them, and re-layouts  10.1 us (3%)
  matrix products  9.34 us (3%)
  starting transfers between devices  8.86 us (3%)
  other arithmetic  3.31 us (1%)
    all_gather x1, blocking collectives, shards(): expert_load = jnp.sum(lax.all_gather(routed_mass, 'exp'), axis=0)  170 us
    all_to_all x1, blocking collectives, shards(): lax.all_to_all(outgoing, 'exp', split_axis=0, concat_axis=0, tiled=True)  108 us
    all_to_all x1, starting transfers between devices, shards(): lax.all_to_all(expert_rows(arrived, gate_weight, up_weight, down_weight),...  8.86 us
  transfers between devices with their start and end apart: 1, of which 0 were waited for; matrix products, arithmetic and copies ran while one was open for 1% of the time, Pallas kernels for 0%

profile of v1, /device:TPU:1, one launch (start us, length us, event | category | flops | bytes accessed | tf_op | source)
XLA Modules:
  0.0 310.5 jit_solution(9572112601727017249)
XLA Ops:
  0.6 0.0 copy-start
  0.7 0.1 eq.45
  0.7 1.0 iota_compare_fusion
  1.8 0.1 copy.23
  1.8 0.1 reduce_window_sum.11
  1.9 0.1 copy.24
  2.0 1.2 convolution_convert_fusion.1
  3.2 0.9 broadcast_in_dim.61
  4.2 108.1 %all_to_all.10 = bf16[128,2,3584]{2,1,0:T(2,128)(2,1)} all-to-all(bf16[128,2,3584]{2,1,0:T(2,128)(2,1)S(1)} %bitcast.23), channel_id=1, replica_groups=mesh['rep'=4,'exp'=128] {'exp'}, dimensions={0} | all-to-all | bytes 3670016 | tf_op jit(solution)/shard_map/all_to_all | solution.py:46
  112.3 4.1 %reshape.38 = bf16[256,3584]{1,0:T(8,128)(2,1)S(1)} reshape(bf16[128,2,3584]{2,1,0:T(2,128)(2,1)} %all_to_all.10) | data formatting | bytes 3670016 | tf_op jit(solution)/shard_map/reshape | solution.py:13
  116.4 1.8 fusion.25
  118.2 0.0 copy-done
  118.2 3.6 %convolution_convert_fusion = bf16[256,3584]{1,0:T(8,128)(2,1)} fusion(bf16[128,3584]{1,0:T(8,128)(2,1)S(1)} %copy-done, bf16[256,3584]{1,0:T(8,128)(2,1)S(1)} %reshape.38, bf16[3584,128]{1,0:T(8,128)(2,1)} %param.10, f32[256,128]{1,0:T(8,128)S(1)} %fusion.25), kind=kOutput, calls=%fused_computation | convolution fusion | flops 470876160 | bytes 5636096 | tf_op jit(solution)/shard_map/dot_general | solution.py:17
  121.8 4.7 %reshape.39 = bf16[128,2,3584]{2,1,0:T(2,128)(2,1)} reshape(bf16[256,3584]{1,0:T(8,128)(2,1)} %convolution_convert_fusion) | data formatting | bytes 3670016 | tf_op jit(solution)/shard_map/reshape | solution.py:20
  126.6 0.0 copy-start.1
  126.6 0.0 copy-start.2
  126.6 8.9 %all-to-all-start.1 = ((bf16[128,2,3584]{2,1,0:T(2,128)(2,1)}), bf16[128,2,3584]{2,1,0:T(2,128)(2,1)S(1)}, u32[]{:S(2)}, u32[]{:S(2)}) async-start(bf16[128,2,3584]{2,1,0:T(2,128)(2,1)} %reshape.39), calls=%async_computation.1 | async-start | bytes 3670016 | tf_op jit(solution)/shard_map/all_to_all | solution.py:47
  135.4 0.0 copy-done.1
  135.4 0.0 copy-done.2
  135.4 1.5 fusion.4
  136.9 170.1 %all-gather.1 = f32[128,1,384]{2,1,0:T(1,128)S(1)} all-gather(f32[1,1,384]{2,1,0:T(1,128)S(1)} %fusion.4), channel_id=2, replica_groups=mesh['rep'=4,'exp'=128] {'exp'}, dimensions={0}, use_global_device_ids=true | all-gather | bytes 198144 | tf_op jit(solution)/shard_map/all_gather | solution.py:32
  307.0 0.8 reduce_sum.29
  307.8 0.0 all-to-all-done.1
  307.8 1.5 convert_reduce_fusion
  309.3 1.3 fusion
  (10 shorter events, 0.1 us)
Async XLA Ops:
  0.6 117.6 %copy-start = (bf16[128,3584]{1,0:T(8,128)(2,1)S(1)}, bf16[128,3584]{1,0:T(8,128)(2,1)}, u32[]{:S(2)}) copy-start(bf16[128,3584]{1,0:T(8,128)(2,1)} %param.11) | copy-start | bytes 2752516
  126.6 8.9 %copy-start.1 = (s32[32,8]{0,1:T(8,128)S(1)}, s32[32,8]{0,1:T(8,128)}, u32[]{:S(2)}) copy-start(s32[32,8]{0,1:T(8,128)} %param.7) | copy-start | bytes 3076
  126.6 8.9 %copy-start.2 = (f32[32,8]{0,1:T(8,128)S(1)}, f32[32,8]{0,1:T(8,128)}, u32[]{:S(2)}) copy-start(f32[32,8]{0,1:T(8,128)} %param.8) | copy-start | bytes 3076
  126.6 181.2 %all-to-all-start.1 = ((bf16[128,2,3584]{2,1,0:T(2,128)(2,1)}), bf16[128,2,3584]{2,1,0:T(2,128)(2,1)S(1)}, u32[]{:S(2)}, u32[]{:S(2)}) async-start(bf16[128,2,3584]{2,1,0:T(2,128)(2,1)} %reshape.39), calls=%async_computation.1 | async-start | bytes 3670016 | tf_op jit(solution)/shard_map/all_to_all | solution.py:47
